TPU v7x, 32 devices: a whole 2x2x4 slice. The times are simulated.
32 devices in a mesh: row: 8 (over z, core), col: 4 (over y, x).
Axes of the slice: x: 2, y: 2, z: 4, core: 2. Of those that a mesh axis runs over, the one named last changes fastest.
Arguments:
- shot_traces: float32 [16384, 2, 8192], P(('row', 'col')), may hold values from -0.046875 to 0.046875
- shot_ids: int32 [16384], P(('row', 'col')), may hold values from 0 to 8191, as said below
- shot_counts: int32 [32], P(('row', 'col')), may hold values from 0 to 512, as said below
- missing_blocks: int32 [64, 64], P('row', 'col'), may hold values from 0 to 1, as said below
- weight_bins: int32 [8192], P(('row', 'col')), may hold values from 0 to 63
- weight_table: float32 [64], replicated, may hold values from 0.1 to 1
- focus_panel: float32 [2, 8192, 512], P(None, ('col', 'row')), may hold values from -6 to 6
Outputs:
- wavefield: float32 [2, 8192, 512], P(None, ('row', 'col'))
- adjoint_image: float32 [2, 8192, 512], P(None, ('col', 'row'))
Inputs may be any that keep to these rules, and one draw needn't show every extreme that they name: `shot_ids`: over the counted slots of all devices every source appears exactly once; uncounted slots hold arbitrary sources. The counted slots of one device hold at most 64 sources of any block of 1024 consecutive sources, and at most (128) of any block of 2048; some device reaches both. `shot_counts`: some device has all 512 slots counted. `missing_blocks`: diagonal blocks are recorded, and of two mirrored blocks at most one is missing.
All inputs are finite; a program needn't handle non-finite values.
Results may differ from a plain program's by a relative error of at most 0.00007.
Values sent between devices are 32-bit elements; how exact they have to be, the bound alone decides.
A program may use at most 320 MiB of HBM per device.

v0:
```python
import jax
import jax.numpy as jnp
from jax import lax
from jax.sharding import PartitionSpec as P


def high_dot(left, right):
    return jnp.dot(left, right, precision=lax.Precision.HIGHEST, preferred_element_type=jnp.float32)


def trans_dot(left, right):
    return lax.dot_general(
        left,
        right,
        (((0,), (0,)), ((), ())),
        precision=lax.Precision.HIGHEST,
        preferred_element_type=jnp.float32,
    )


def pack_slots(traces, labels, held_count, group_size, group_count, capacity):
    slot_total = labels.shape[0]
    slot_index = jnp.arange(slot_total, dtype=jnp.int32)
    is_used = slot_index < held_count
    dest_group = labels // group_size
    onehot = (
        (dest_group[:, None] == jnp.arange(group_count, dtype=jnp.int32)[None, :])
        & is_used[:, None]
    ).astype(jnp.int32)
    before = jnp.cumsum(onehot, axis=0) - onehot
    rank_in = jnp.sum(before * onehot, axis=1)
    position = jnp.where(is_used, dest_group * capacity + rank_in, group_count * capacity)
    source = (
        jnp.full((group_count * capacity,), slot_total, jnp.int32)
        .at[position]
        .set(slot_index, mode="drop")
    )
    packed = jnp.take(traces, source, axis=0, mode="fill", fill_value=0.0)
    packed_labels = jnp.take(labels, source, axis=0, mode="fill", fill_value=-1)
    return (packed, packed_labels)


def place_rows(arrived, labels, first_label, length):
    has_label = labels >= 0
    target = jnp.where(has_label, labels - first_label, length)
    source = (
        jnp.zeros((length,), jnp.int32)
        .at[target]
        .set(jnp.arange(labels.shape[0], dtype=jnp.int32), mode="drop")
    )
    return jnp.take(arrived, source, axis=0)


def lookup(bins, table):
    matches = bins[:, None] == jnp.arange(table.shape[0], dtype=jnp.int32)[None, :]
    return jnp.sum(jnp.where(matches, table[None, :], 0.0), axis=1)


def local(
    shot_traces, shot_ids, shot_counts, missing_blocks, weight_bins, weight_table, focus_panel
):
    slot_total = shot_traces.shape[0]
    stations = shot_traces.shape[2]
    row_count = lax.axis_size("row")
    col_count = lax.axis_size("col")
    src_tile = stations // row_count
    rcv_tile = stations // col_count
    row_index = lax.axis_index("row")
    col_index = lax.axis_index("col")
    held_count = shot_counts[0]
    packed, packed_labels = pack_slots(
        shot_traces, shot_ids, held_count, src_tile, row_count, slot_total // row_count
    )
    outgoing = packed.reshape(slot_total, 2, col_count, rcv_tile)
    label_copies = jnp.broadcast_to(packed_labels[:, None, None], (slot_total, 1, col_count))
    arrived, arrived_labels = (
        lax.all_to_all(
            lax.all_to_all(outgoing, "row", split_axis=0, concat_axis=0, tiled=True),
            "col",
            split_axis=2,
            concat_axis=0,
            tiled=True,
        ),
        lax.all_to_all(
            lax.all_to_all(label_copies, "row", split_axis=0, concat_axis=0, tiled=True),
            "col",
            split_axis=2,
            concat_axis=0,
            tiled=True,
        ),
    )
    direct = place_rows(
        arrived.reshape(-1, 2, rcv_tile), arrived_labels.reshape(-1), row_index * src_tile, src_tile
    )
    capacity_rec = slot_total // col_count
    packed_mirror, mirror_labels = pack_slots(
        shot_traces, shot_ids, held_count, rcv_tile, col_count, capacity_rec
    )
    mirror_out = packed_mirror.reshape(slot_total, 2, row_count, src_tile)
    mirror_copies = jnp.broadcast_to(mirror_labels[:, None, None], (slot_total, 1, row_count))
    halfway, halfway_labels = (
        lax.all_to_all(mirror_out, "row", split_axis=2, concat_axis=0, tiled=True),
        lax.all_to_all(mirror_copies, "row", split_axis=2, concat_axis=0, tiled=True),
    )
    halfway = halfway.reshape(row_count, col_count, capacity_rec, 2, src_tile)
    halfway_labels = halfway_labels.reshape(row_count, col_count, capacity_rec)
    mirrored, mirrored_labels = (
        lax.all_to_all(halfway, "col", split_axis=1, concat_axis=0, tiled=True),
        lax.all_to_all(halfway_labels, "col", split_axis=1, concat_axis=0, tiled=True),
    )
    transposed = place_rows(
        mirrored.reshape(-1, 2, src_tile),
        mirrored_labels.reshape(-1),
        col_index * rcv_tile,
        rcv_tile,
    )
    blocks_down = missing_blocks.shape[0]
    blocks_across = missing_blocks.shape[1]
    block_size = src_tile // blocks_down
    is_missing = jnp.broadcast_to(
        missing_blocks[:, None, :, None] > 0, (blocks_down, block_size, blocks_across, block_size)
    ).reshape(src_tile, rcv_tile)
    kernel_re = jnp.where(is_missing, transposed[:, 0, :].T, direct[:, 0, :])
    kernel_im = jnp.where(is_missing, transposed[:, 1, :].T, direct[:, 1, :])
    focus_all = lax.all_gather(focus_panel, "row", axis=1, tiled=True)
    panel_re = focus_all[0]
    panel_im = focus_all[1]
    field_re = high_dot(kernel_re, panel_re) - high_dot(kernel_im, panel_im)
    field_im = high_dot(kernel_re, panel_im) + high_dot(kernel_im, panel_re)
    own_rows = lax.psum_scatter(
        jnp.stack([field_re, field_im], axis=1), "col", scatter_dimension=0, tiled=True
    )
    weighted = own_rows * lookup(weight_bins, weight_table)[:, None, None]
    weighted_all = lax.all_gather(weighted, "col", axis=0, tiled=True)
    weighted_re = weighted_all[:, 0, :]
    weighted_im = weighted_all[:, 1, :]
    image_re = trans_dot(kernel_re, weighted_re) + trans_dot(kernel_im, weighted_im)
    image_im = trans_dot(kernel_re, weighted_im) - trans_dot(kernel_im, weighted_re)
    image_rows = lax.psum_scatter(
        jnp.stack([image_re, image_im], axis=1), "row", scatter_dimension=0, tiled=True
    )
    return (jnp.swapaxes(own_rows, 0, 1), jnp.swapaxes(image_rows, 0, 1))


def solution(mesh):
    placed = (
        P(("row", "col"), None, None),
        P(("row", "col")),
        P(("row", "col")),
        P("row", "col"),
        P(("row", "col")),
        P(),
        P(None, ("col", "row"), None),
    )
    return jax.shard_map(
        local,
        mesh=mesh,
        in_specs=placed,
        out_specs=(P(None, ("row", "col"), None), P(None, ("col", "row"), None)),
        check_vma=False,
    )
```

profile of v0, /device:TPU:2, one launch (start us, length us, event | category | flops | bytes accessed | tf_op | source)
XLA Modules:
  0.0 3003.1 jit_solution(7320027503806781261)
XLA Ops:
  48.7 44.3 %gather_fusion.3 = f32[512,2,8192]{2,1,0:T(2,128)} fusion(f32[512,2,8192]{2,1,0:T(2,128)} %param.11, s32[1024]{0:T(1024)S(1)} %pad_clamp_fusion.1), kind=kCustom, calls=%fused_computation.1.clone | custom fusion | bytes 67110912 | tf_op jit(solution)/shard_map/jit(_take)/gather | solution.py:38
  99.1 24.2 broadcast_select_fusion.1
  123.3 48.8 %copy.56 = f32[512,2,8192]{0,2,1:T(8,128)} copy(f32[512,2,8192]{2,1,0:T(2,128)} %broadcast_select_fusion.1) | data formatting | bytes 67108864 | tf_op jit(solution)/shard_map/jit(_take)/select_n | solution.py:38
  172.0 22.9 copy.57
  202.8 44.4 %gather_fusion.5 = f32[512,2,8192]{2,1,0:T(2,128)} fusion(f32[512,2,8192]{2,1,0:T(2,128)} %param.11, s32[1024]{0:T(1024)S(1)} %pad_clamp_fusion), kind=kCustom, calls=%fused_computation.3.clone | custom fusion | bytes 67110912 | tf_op jit(solution)/shard_map/jit(_take)/gather | solution.py:38
  247.3 24.2 broadcast_select_fusion
  271.4 48.7 %copy.64 = f32[512,2,8192]{0,2,1:T(8,128)} copy(f32[512,2,8192]{2,1,0:T(2,128)} %broadcast_select_fusion) | data formatting | bytes 67108864 | tf_op jit(solution)/shard_map/jit(_take)/select_n | solution.py:38
  320.2 39.8 %copy.65 = f32[512,2,4,2048]{3,2,1,0:T(4,128)} copy(f32[512,2,4,2048]{0,3,2,1:T(8,128)} %bitcast.133) | data formatting | bytes 67108864 | tf_op jit(solution)/shard_map/reshape | solution.py:74
  360.0 566.0 %all-to-all-done.2 = f32[512,2,8,1024]{0,3,1,2:T(8,128)} async-done(((f32[512,2,8,1024]{0,3,1,2:T(8,128)}), f32[512,2,8,1024]{0,3,1,2:T(8,128)}, u32[]{:S(2)}, u32[]{:S(2)}) %all-to-all-start.2) | async-done | bytes 33554464 | tf_op jit(solution)/shard_map/all_to_all | solution.py:102
  933.1 31.9 %copy.58 = f32[512,2,8,1024]{3,0,1,2:T(8,128)} copy(f32[512,2,8,1024]{0,3,1,2:T(8,128)} %all-to-all-done.2) | data formatting | bytes 67108864 | tf_op jit(solution)/shard_map/all_to_all | solution.py:102
  965.0 23.4 copy.59
  988.4 667.9 %all-to-all-done.6 = f32[512,2,4,2048]{3,2,1,0:T(4,128)} async-done(((f32[512,2,4,2048]{3,2,1,0:T(4,128)}), f32[512,2,4,2048]{3,2,1,0:T(4,128)}, u32[]{:S(2)}, u32[]{:S(2)}) %all-to-all-start.6) | async-done | bytes 33554464 | tf_op jit(solution)/shard_map/all_to_all | solution.py:78
  1666.0 37.9 %copy.66 = f32[512,2,4,2048]{0,3,1,2:T(8,128)} copy(f32[512,2,4,2048]{3,2,1,0:T(4,128)} %all-to-all-done.6) | data formatting | bytes 67108864 | tf_op jit(solution)/shard_map/all_to_all | solution.py:78
  1703.9 323.8 %all-to-all-done.3 = f32[8,4,128,2,1024]{4,2,3,0,1:T(8,128)} async-done(((f32[8,4,128,2,1024]{4,2,3,0,1:T(8,128)}), f32[8,4,128,2,1024]{4,2,3,0,1:T(8,128)}, u32[]{:S(2)}, u32[]{:S(2)}) %all-to-all-start.3) | async-done | bytes 33554464 | tf_op jit(solution)/shard_map/all_to_all | solution.py:108
  2047.0 15.9 scatter_custom_fusion.1
  2063.0 23.5 copy.60
  2086.5 55.0 %copy.61 = f32[4096,2,1024]{2,1,0:T(2,128)} copy(f32[4096,2,1024]{2,0,1:T(8,128)} %bitcast.135) | data formatting | bytes 67108864 | tf_op jit(solution)/shard_map/reshape | solution.py:112
  2141.5 257.5 %all-to-all-done.7 = f32[512,2,4,2048]{0,3,1,2:T(8,128)} async-done(((f32[512,2,4,2048]{0,3,1,2:T(8,128)}), f32[512,2,4,2048]{0,3,1,2:T(8,128)}, u32[]{:S(2)}, u32[]{:S(2)}) %all-to-all-start.7) | async-done | bytes 33554464 | tf_op jit(solution)/shard_map/all_to_all | solution.py:77
  2398.9 31.8 %copy.67 = f32[512,2,4,2048]{3,0,2,1:T(8,128)} copy(f32[512,2,4,2048]{0,3,1,2:T(8,128)} %all-to-all-done.7) | data formatting | bytes 67108864 | tf_op jit(solution)/shard_map/all_to_all | solution.py:77
  2430.7 55.0 %copy.68 = f32[2048,2,2048]{2,1,0:T(2,128)} copy(f32[2048,2,2048]{2,0,1:T(8,128)} %bitcast.136) | data formatting | bytes 67108864 | tf_op jit(solution)/shard_map/reshape | solution.py:93
  2485.8 39.4 %gather_fusion.1 = f32[1024,2,2048]{2,1,0:T(2,128)} fusion(f32[2048,2,2048]{2,1,0:T(2,128)} %copy.68, s32[1024]{0:T(1024)S(1)} %fusion.22), kind=kCustom, calls=%fused_computation.5 | custom fusion | bytes 33558528 | tf_op jit(solution)/shard_map/jit(_take)/gather | solution.py:51
  2525.2 25.0 copy.69
  2550.2 54.2 %gather_fusion = f32[2048,2,1024]{2,1,0:T(2,128)} fusion(f32[4096,2,1024]{2,1,0:T(2,128)} %copy.61, s32[2048]{0:T(1024)S(1)} %fusion.19), kind=kCustom, calls=%fused_computation.4 | custom fusion | bytes 33562624 | tf_op jit(solution)/shard_map/jit(_take)/gather | solution.py:51
  2634.0 19.2 fusion.31
  2653.8 17.8 fusion.1
  2671.7 16.7 fusion.3
  2732.2 51.4 %reduce-scatter.3.cloned.1.call-done = f32[256,2,512]{2,0,1:T(8,128)} async-done(((f32[1024,2,512]{2,0,1:T(8,128)}), f32[256,2,512]{2,0,1:T(8,128)}) %reduce-scatter.3.cloned.1.call-update) | async-done | bytes 1048592 | tf_op jit(solution)/shard_map/reduce_scatter | solution.py:130
  2786.0 52.7 %all-gather.5.cloned.1.call-done = f32[1024,2,512]{2,0,1:T(8,128)} async-done(((f32[256,2,512]{2,0,1:T(8,128)}), f32[1024,2,512]{2,0,1:T(8,128)}) %all-gather.5.cloned.1.call-update) | async-done | bytes 4194320 | tf_op jit(solution)/shard_map/all_gather | solution.py:134
  2838.7 17.2 fusion.6
  2856.0 16.0 fusion.7
  2887.1 15.1 subtract_bitcast_fusion
  2906.5 89.7 %reduce-scatter.5.cloned.1.call-done = f32[256,2,512]{2,0,1:T(8,128)} async-done(((f32[2048,2,512]{2,0,1:T(8,128)}), f32[256,2,512]{2,0,1:T(8,128)}) %reduce-scatter.5.cloned.1.call-update) | async-done | bytes 1048592 | tf_op jit(solution)/shard_map/reduce_scatter | solution.py:139
  (114 shorter events, 186.4 us)
Async XLA Ops:
  22.1 11.0 all-to-all-start.4
  33.7 10.7 all-to-all-start
  44.4 49.2 %all-to-all-start.5 = ((s32[512,1,4]{0,1,2:T(1,128)}), s32[512,1,4]{0,1,2:T(1,128)S(1)}, u32[]{:S(2)}, u32[]{:S(2)}) async-start(s32[512,1,4]{0,1,2:T(1,128)} %copy.63), calls=%async_computation.5 | async-start | bytes 16384 | tf_op jit(solution)/shard_map/all_to_all | solution.py:84
  93.6 0.6 copy-start.5
  94.2 100.7 %all-to-all-start.1 = ((s32[8,4,128]{2,0,1:T(8,128)}), s32[8,4,128]{2,0,1:T(8,128)S(1)}, u32[]{:S(2)}, u32[]{:S(2)}) async-start(s32[8,4,128]{2,0,1:T(8,128)} %bitcast.127), calls=%async_computation.1 | async-start | bytes 32768 | tf_op jit(solution)/shard_map/all_to_all | solution.py:109
  194.9 0.6 copy-start.3
  195.5 730.5 %all-to-all-start.2 = ((f32[512,2,8,1024]{0,3,1,2:T(8,128)}), f32[512,2,8,1024]{0,3,1,2:T(8,128)}, u32[]{:S(2)}, u32[]{:S(2)}) async-start(f32[512,2,8,1024]{0,3,1,2:T(8,128)} %copy.57), calls=%async_computation.2 | async-start | bytes 67108864 | tf_op jit(solution)/shard_map/all_to_all | solution.py:102
  926.0 730.3 %all-to-all-start.6 = ((f32[512,2,4,2048]{3,2,1,0:T(4,128)}), f32[512,2,4,2048]{3,2,1,0:T(4,128)}, u32[]{:S(2)}, u32[]{:S(2)}) async-start(f32[512,2,4,2048]{3,2,1,0:T(4,128)} %copy.65), calls=%async_computation.6 | async-start | bytes 67108864 | tf_op jit(solution)/shard_map/all_to_all | solution.py:78
  1656.3 371.4 %all-to-all-start.3 = ((f32[8,4,128,2,1024]{4,2,3,0,1:T(8,128)}), f32[8,4,128,2,1024]{4,2,3,0,1:T(8,128)}, u32[]{:S(2)}, u32[]{:S(2)}) async-start(f32[8,4,128,2,1024]{4,2,3,0,1:T(8,128)} %copy.59), calls=%async_computation.3 | async-start | bytes 67108864 | tf_op jit(solution)/shard_map/all_to_all | solution.py:108
  1703.9 334.9 %copy-start.7 = (s32[8,16]{1,0:T(8,128)S(1)}, s32[8,16]{1,0:T(8,128)}, u32[]{:S(2)}) copy-start(s32[8,16]{1,0:T(8,128)} %param.14) | copy-start | bytes 1540
  1703.9 335.0 %copy-start.6 = (s32[512,1,4]{0,1,2:T(1,128)S(1)}, s32[512,1,4]{0,1,2:T(1,128)}, u32[]{:S(2)}) copy-start(s32[512,1,4]{0,1,2:T(1,128)} %copy-done.5) | copy-start | bytes 24580
  1703.9 343.1 %copy-start.4 = (s32[8,4,128]{2,0,1:T(8,128)S(1)}, s32[8,4,128]{2,0,1:T(8,128)}, u32[]{:S(2)}) copy-start(s32[8,4,128]{2,0,1:T(8,128)} %copy-done.3) | copy-start | bytes 49156
  2027.7 371.2 %all-to-all-start.7 = ((f32[512,2,4,2048]{0,3,1,2:T(8,128)}), f32[512,2,4,2048]{0,3,1,2:T(8,128)}, u32[]{:S(2)}, u32[]{:S(2)}) async-start(f32[512,2,4,2048]{0,3,1,2:T(8,128)} %copy.66), calls=%async_computation.7 | async-start | bytes 67108864 | tf_op jit(solution)/shard_map/all_to_all | solution.py:77
  2038.0 633.7 %all-gather.3.cloned.1.call-start = ((), (), s32[]{:S(2)}) async-start(), calls=%async_computation.10 | async-start | bytes 9437184 | tf_op jit(solution)/shard_map/all_gather | solution.py:125
  2038.7 745.0 %reduce-scatter.3.cloned.1.call-start = ((), (), s32[]{:S(2)}) async-start(), calls=%async_computation.11 | async-start | bytes 5242880 | tf_op jit(solution)/shard_map/reduce_scatter | solution.py:130
  2604.4 16.5 copy-start.1
  2671.7 16.7 copy-start
  2671.7 16.8 copy-start.10
  2688.5 27.3 slice-start.2
  2702.2 13.6 slice-start.3
  2729.6 2.5 copy-start.8
  2729.6 2.5 copy-start.9
  2732.0 106.7 %all-gather.5.cloned.1.call-start = ((), (), s32[]{:S(2)}) async-start(), calls=%async_computation.12 | async-start | bytes 5242880 | tf_op jit(solution)/shard_map/all_gather | solution.py:134
  2786.0 210.2 %reduce-scatter.5.cloned.1.call-start = ((), (), s32[]{:S(2)}) async-start(), calls=%async_computation.13 | async-start | bytes 9437184 | tf_op jit(solution)/shard_map/reduce_scatter | solution.py:139
  2838.7 17.3 copy-start.2
  2838.7 33.2 %slice-start = ((s8[8388608]{0:T(1024)(128)(4,1)}), s8[4194304]{0:T(1024)(128)(4,1)S(1)}, s32[]{:S(2)}) async-start(s8[8388608]{0:T(1024)(128)(4,1)} %bitcast.137), calls=%async_computation.14 | async-start | bytes 8388608
  2856.0 16.0 slice-start.1
Sparse Core Ops, SparseCore 0:
  2040.4 81.3 all-gather.2
  2732.1 51.4 reduce-scatter.2
  2786.1 52.5 all-gather.4
  2906.6 89.5 reduce-scatter.4
where the time goes:
time: 3020 us; the launch traced here: 3000 us
  waiting for transfers between devices  2010 us (67%)
  local copies, waits for them, and re-layouts  693 us (23%)
  matrix products  121 us (4%)
  other arithmetic  106 us (4%)
  starting transfers between devices  53.6 us (2%)
    all_to_all x1, waiting for transfers between devices, local(): lax.all_to_all(outgoing, 'row', split_axis=0, concat_axis=0, tiled=True)  668 us
    all_to_all x1, waiting for transfers between devices, local(): lax.all_to_all(mirror_out, 'row', split_axis=2, concat_axis=0, tiled=True)  566 us
    all_to_all x1, waiting for transfers between devices, local(): lax.all_to_all(halfway, 'col', split_axis=1, concat_axis=0, tiled=True)  324 us
    all_to_all x1, waiting for transfers between devices, local(): lax.all_to_all(lax.all_to_all(outgoing, 'row', split_axis=0, concat_axis=...  257 us
    gather x3, local copies, waits for them, and re-layouts, place_rows(): return jnp.take(arrived, source, axis=0)  119 us
    select_n x2, local copies, waits for them, and re-layouts, pack_slots(): packed = jnp.take(traces, source, axis=0, mode='fill', fill_value=0.0)  97.5 us
    reduce_scatter x1, waiting for transfers between devices, local(): lax.psum_scatter(jnp.stack([image_re, image_im], axis=1), 'row', scatter_...  89.7 us
    gather x2, local copies, waits for them, and re-layouts, pack_slots(): packed = jnp.take(traces, source, axis=0, mode='fill', fill_value=0.0)  88.8 us
  transfers between devices with their start and end apart: 12, of which 8 were waited for; matrix products, arithmetic and copies ran while one was open for 26% of the time, Pallas kernels for 0%

commit v1 on v0

v1 whole, which is shorter than its diff:
```python
import functools

import jax
import jax.numpy as jnp
from jax import lax
from jax.experimental import pallas as pl
from jax.experimental.pallas import tpu as pltpu
from jax.sharding import PartitionSpec as P

AXES = ("row", "col")


def partner(i, j, rows):
    half = rows // 2
    if j:
        return (i + j) % rows
    if i < half:
        return i + half if i % 2 == 0 else i - 1
    return i - half if i % 2 else i + 1


def is_diagonal(i, j, rows):
    return j == 0 and (i % 2 == 1) == (i < rows // 2)


def plan(rows, cols):
    table = [[None] * rows for _ in range(rows)]
    firsts, seconds = [], []
    for i in range(rows):
        for j in range(cols):
            p = i * cols + j
            b = partner(i, j, rows)
            diagonal = is_diagonal(i, j, rows)
            table[i][i if diagonal else b] = 2 * p
            table[b][b if diagonal else i] = 2 * p + 1
            firsts.append(i)
            seconds.append(b)
    total = rows * cols
    assert all(entry is not None for line in table for entry in line)
    to_partner = [(p, seconds[p] * cols + p % cols) for p in range(total)]
    from_partner = [(b, a) for a, b in to_partner]
    to_col_major = [(m, (m % rows) * cols + m // rows) for m in range(total)]
    to_row_major = [(b, a) for a, b in to_col_major]
    return table, firsts, seconds, to_partner, from_partner, to_col_major, to_row_major


def dot(left, right):
    return jnp.dot(left, right, precision=lax.Precision.HIGH, preferred_element_type=jnp.float32)


def trans_dot(left, right):
    return lax.dot_general(
        left,
        right,
        (((0,), (0,)), ((), ())),
        precision=lax.Precision.HIGH,
        preferred_element_type=jnp.float32,
    )


def pack_kernel(table, cap, width, src_ref, x_ref, o_ref, buf, in_sem, out_sem):
    count = len(table)

    def fetch(t):
        s = t % 2

        def one(k, carry):
            pltpu.make_async_copy(
                x_ref.at[src_ref[t * cap + k]], buf.at[s, k], in_sem.at[s]
            ).start()
            return carry

        lax.fori_loop(0, cap, one, 0)

    def outs(t):
        s = t % 2
        return [
            pltpu.make_async_copy(
                buf.at[s, :, :, pl.ds(c * width, width)], o_ref.at[table[t][c]], out_sem.at[s, c]
            )
            for c in range(count)
        ]

    fetch(0)
    for t in range(count):
        s = t % 2
        if t + 1 < count:
            if t >= 1:
                for copy in outs(t - 1):
                    copy.wait()
            fetch(t + 1)
        pltpu.make_async_copy(x_ref.at[pl.ds(0, cap)], buf.at[s], in_sem.at[s]).wait()
        for copy in outs(t):
            copy.start()
    for t in range(max(count - 2, 0), count):
        for copy in outs(t):
            copy.wait()


def pack(traces, source, table, cap, width):
    count = len(table)
    return pl.pallas_call(
        functools.partial(pack_kernel, table, cap, width),
        grid_spec=pltpu.PrefetchScalarGridSpec(
            num_scalar_prefetch=1,
            grid=(1,),
            in_specs=[pl.BlockSpec(memory_space=pl.ANY)],
            out_specs=pl.BlockSpec(memory_space=pl.ANY),
            scratch_shapes=[
                pltpu.VMEM((2, cap, 2, count * width), jnp.float32),
                pltpu.SemaphoreType.DMA((2,)),
                pltpu.SemaphoreType.DMA((2, count)),
            ],
        ),
        out_shape=jax.ShapeDtypeStruct((count * count, cap, 2, width), jnp.float32),
    )(source, traces)


def slot_sources(labels, held_count, group_size, group_count, capacity):
    slot_total = labels.shape[0]
    slot_index = jnp.arange(slot_total, dtype=jnp.int32)
    is_used = slot_index < held_count
    dest_group = labels // group_size
    onehot = (
        (dest_group[:, None] == jnp.arange(group_count, dtype=jnp.int32)[None, :])
        & is_used[:, None]
    ).astype(jnp.int32)
    before = jnp.cumsum(onehot, axis=0) - onehot
    rank_in = jnp.sum(before * onehot, axis=1)
    place = jnp.where(is_used, dest_group * capacity + rank_in, group_count * capacity)
    hit = place[None, :] == jnp.arange(group_count * capacity, dtype=jnp.int32)[:, None]
    source = jnp.sum(jnp.where(hit, slot_index[None, :], 0), axis=1)
    packed_labels = jnp.sum(jnp.where(hit, labels[None, :] + 1, 0), axis=1) - 1
    return source, packed_labels


def row_sources(labels, first_label, length, indices):
    target = jnp.where(labels >= 0, labels - first_label, length)
    return jnp.zeros((length,), jnp.int32).at[target].set(indices, mode="drop")


def lookup(bins, table):
    matches = bins[:, None] == jnp.arange(table.shape[0], dtype=jnp.int32)[None, :]
    return jnp.sum(jnp.where(matches, table[None, :], 0.0), axis=1)


def local(
    shot_traces, shot_ids, shot_counts, missing_blocks, weight_bins, weight_table, focus_panel
):
    slot_total = shot_traces.shape[0]
    stations = shot_traces.shape[2]
    focus = focus_panel.shape[2]
    rows = lax.axis_size("row")
    cols = lax.axis_size("col")
    assert rows == 2 * cols and rows % 4 == 0
    devices = rows * cols
    width = stations // rows
    cap = slot_total // rows
    i = lax.axis_index("row")
    j = lax.axis_index("col")
    me = i * cols + j
    table, firsts, seconds, to_partner, from_partner, to_col_major, to_row_major = plan(rows, cols)
    first = i
    second = jnp.asarray(seconds, jnp.int32)[me]
    diagonals = [is_diagonal(p // cols, p % cols, rows) for p in range(devices)]
    diagonal = jnp.asarray(diagonals, jnp.bool_)[me]
    col_first = jnp.where(diagonal, first, second)
    col_second = jnp.where(diagonal, second, first)

    source, packed_labels = slot_sources(shot_ids, shot_counts[0], width, rows, cap)
    by_group = packed_labels.reshape(rows, cap)
    label_out = jnp.stack(
        [by_group[jnp.asarray(firsts, jnp.int32)], by_group[jnp.asarray(seconds, jnp.int32)]],
        axis=1,
    )
    labels = lax.all_to_all(label_out, AXES, split_axis=0, concat_axis=0, tiled=True)
    packed = pack(shot_traces, source, table, cap, width)
    arrived = lax.all_to_all(
        packed.reshape(devices, 2, cap, 2, width), AXES, split_axis=0, concat_axis=0, tiled=True
    ).reshape(devices * 2 * cap, 2, width)
    indices = jnp.arange(devices * 2 * cap, dtype=jnp.int32).reshape(devices, 2, cap)

    def block(q, group):
        where_from = row_sources(
            labels[:, q].reshape(-1), group * width, width, indices[:, q].reshape(-1)
        )
        taken = jnp.take(arrived, where_from, axis=0, mode="clip")
        return taken[:, 0, :], taken[:, 1, :]

    re0, im0 = block(0, first)
    re1, im1 = block(1, second)

    missing = lax.all_gather(missing_blocks, "row", axis=0, tiled=True)
    missing = lax.all_gather(missing, "col", axis=1, tiled=True)
    blocks = missing.shape[0] // rows
    side = width // blocks

    def mask_of(group, col_group):
        part = lax.dynamic_slice(missing, (group * blocks, col_group * blocks), (blocks, blocks))
        return jnp.broadcast_to(
            part[:, None, :, None] > 0, (blocks, side, blocks, side)
        ).reshape(width, width)

    mask0 = mask_of(first, col_first)
    mask1 = mask_of(second, col_second)

    def fill(mask, own, other):
        return jnp.where(mask, jnp.where(diagonal, own, other).T, own)

    full_re0, full_im0 = fill(mask0, re0, re1), fill(mask0, im0, im1)
    full_re1, full_im1 = fill(mask1, re1, re0), fill(mask1, im1, im0)

    panel = jnp.concatenate([focus_panel[0], focus_panel[1]], axis=1)
    panel = lax.ppermute(panel, AXES, to_row_major)
    panel_first = lax.all_gather(panel, "col", axis=0, tiled=True)
    panel_second = lax.ppermute(panel_first, AXES, from_partner)

    def forward(re, im, vec):
        turned = jnp.concatenate([-vec[:, focus:], vec[:, :focus]], axis=1)
        return dot(re, vec) + dot(im, turned)

    def backward(re, im, vec):
        turned = jnp.concatenate([vec[:, focus:], -vec[:, :focus]], axis=1)
        return trans_dot(re, vec) + trans_dot(im, turned)

    field_second = forward(
        full_re1, full_im1, jnp.where(diagonal, panel_second, panel_first)
    )
    field_moved = lax.ppermute(field_second, AXES, to_partner)
    field_first = forward(full_re0, full_im0, jnp.where(diagonal, panel_first, panel_second))
    own = lax.psum_scatter(field_first + field_moved, "col", scatter_dimension=0, tiled=True)
    weighted = own * lookup(weight_bins, weight_table)[:, None]
    weighted_first = lax.all_gather(weighted, "col", axis=0, tiled=True)
    weighted_second = lax.ppermute(weighted_first, AXES, from_partner)
    image0 = backward(full_re0, full_im0, weighted_first)
    image1 = backward(full_re1, full_im1, weighted_second)
    image_moved = lax.ppermute(jnp.where(diagonal, image1, image0), AXES, to_partner)
    image_sum = jnp.where(diagonal, image0, image1) + image_moved
    image = lax.psum_scatter(image_sum, "col", scatter_dimension=0, tiled=True)
    image = lax.ppermute(image, AXES, to_col_major)
    return (
        jnp.stack([own[:, :focus], own[:, focus:]]),
        jnp.stack([image[:, :focus], image[:, focus:]]),
    )


def solution(mesh):
    placed = (
        P(("row", "col"), None, None),
        P(("row", "col")),
        P(("row", "col")),
        P("row", "col"),
        P(("row", "col")),
        P(),
        P(None, ("col", "row"), None),
    )
    return jax.shard_map(
        local,
        mesh=mesh,
        in_specs=placed,
        out_specs=(P(None, ("row", "col"), None), P(None, ("col", "row"), None)),
        check_vma=False,
    )
```

time: 3020 us -> 1890 us (0.63)
  waiting for transfers between devices: 2010 us -> 1390 us
  local copies, waits for them, and re-layouts: 693 us -> 147 us
  blocking collectives: 0 us -> 147 us
  matrix products: 121 us -> 59.9 us
  other arithmetic: 106 us -> 60.9 us
  Pallas kernels: 0 us -> 42 us
  starting transfers between devices: 53.6 us -> 19.6 us
    all_to_all x8 -> x2, waiting for transfers between devices: 1820 us -> 0.01 us  [the longest x1 0.01 us: local(): lax.all_to_all(label_out, AXES, split_axis=0, concat_axis=0, tiled=True)]
    ppermute x0 -> x6, waiting for transfers between devices: none -> 690 us  [the longest x1 574 us: local(): panel = lax.ppermute(panel, AXES, to_row_major)]
    all_gather x2, waiting for transfers between devices: 52.7 us -> 339 us  [the longest x1 287 us: local(): panel_first = lax.all_gather(panel, 'col', axis=0, tiled=True)]
    reduce_scatter x2, waiting for transfers between devices: 141 us -> 360 us  [the longest x1 226 us: local(): image = lax.psum_scatter(image_sum, 'col', scatter_dimension=0, tiled=True)]
    reshape x5 -> x0, local copies, waits for them, and re-layouts: 196 us -> none  [the longest x1 55 us: local(): mirrored.reshape(-1, 2, src_tile)]
    gather x7 -> x4, local copies, waits for them, and re-layouts: 215 us -> 55.9 us  [the longest x2 54.7 us: block(): taken = jnp.take(arrived, where_from, axis=0, mode='clip')]
    all_gather x0 -> x2, blocking collectives: none -> 147 us  [the longest x1 96 us: local(): missing = lax.all_gather(missing, 'col', axis=1, tiled=True)]
    all_to_all x5 -> x1, local copies, waits for them, and re-layouts: 126 us -> 0.51 us  [local(): lax.all_to_all(label_out, AXES, split_axis=0, concat_axis=0, tiled=True)]
  transfers between devices with their start and end apart: 12 -> 12, of which waited for: 8 -> 8; matrix products, arithmetic and copies ran while one was open for 26% -> 5% of each run, Pallas kernels for 0% -> 2%
where the time goes in v1:
time: 1890 us; the launch traced here: 1880 us
  waiting for transfers between devices  1390 us (74%)
  local copies, waits for them, and re-layouts  147 us (8%)
  blocking collectives  147 us (8%)
  other arithmetic  60.9 us (3%)
  matrix products  59.9 us (3%)
  Pallas kernels  42 us (2%)
  starting transfers between devices  19.6 us (1%)
  between operations  19.1 us (1%)
    ppermute x1, waiting for transfers between devices, local(): panel = lax.ppermute(panel, AXES, to_row_major)  574 us
    all_gather x1, waiting for transfers between devices, local(): panel_first = lax.all_gather(panel, 'col', axis=0, tiled=True)  287 us
    reduce_scatter x1, waiting for transfers between devices, local(): image = lax.psum_scatter(image_sum, 'col', scatter_dimension=0, tiled=True)  226 us
    reduce_scatter x1, waiting for transfers between devices, local(): lax.psum_scatter(field_first + field_moved, 'col', scatter_dimension=0, t...  134 us
    all_gather x1, blocking collectives, local(): missing = lax.all_gather(missing, 'col', axis=1, tiled=True)  96 us
    gather x2, local copies, waits for them, and re-layouts, block(): taken = jnp.take(arrived, where_from, axis=0, mode='clip')  54.7 us
    all_gather x1, waiting for transfers between devices, local(): weighted_first = lax.all_gather(weighted, 'col', axis=0, tiled=True)  52.7 us
    all_gather x1, blocking collectives, local(): missing = lax.all_gather(missing_blocks, 'row', axis=0, tiled=True)  50.5 us
  transfers between devices with their start and end apart: 12, of which 8 were waited for; matrix products, arithmetic and copies ran while one was open for 5% of the time, Pallas kernels for 2%

profile of v1, /device:TPU:2, one launch (start us, length us, event | category | flops | bytes accessed | tf_op | source)
XLA Modules:
  0.0 1883.6 jit_solution(1913393230460932010)
XLA Ops:
  20.4 42.0 %shard_map.122 = f32[64,64,2,1024]{3,2,1,0:T(2,128)} custom-call(s32[512]{0:T(512)} %get-tuple-element.7.src_ref, f32[512,2,8192]{2,1,0:T(2,128)} %x_ref.1), custom_call_target="tpu_custom_call" | custom-call | tf_op jit(solution)/shard_map/pallas_call | solution.py:102
  68.9 573.8 %collective-permute-done = f32[256,1024]{1,0:T(8,128)S(1)} collective-permute-done((f32[256,1024]{1,0:T(8,128)S(1)}, f32[256,1024]{1,0:T(8,128)S(1)}, u32[]{:S(2)}, u32[]{:S(2)}) %collective-permute-start) | collective-permute-done | bytes 1048608 | tf_op jit(solution)/shard_map/ppermute | solution.py:214
  643.7 286.8 %all-gather.3.cloned.1.call-done = f32[1024,1024]{1,0:T(8,128)} async-done(((f32[256,1024]{1,0:T(8,128)}), f32[1024,1024]{1,0:T(8,128)}) %all-gather.3.cloned.1.call-update) | async-done | bytes 4194320 | tf_op jit(solution)/shard_map/all_gather | solution.py:215
  938.2 50.5 %all_gather.12 = s32[64,16]{1,0:T(8,128)S(1)} all-gather(s32[8,16]{1,0:T(8,128)S(1)} %copy-done.17), channel_id=1, replica_groups=mesh['row'=8,'col'=4] {'row'}, dimensions={0}, use_global_device_ids=true | all-gather | bytes 4608 | tf_op jit(solution)/shard_map/all_gather | solution.py:193
  988.7 96.0 %all_gather.13 = s32[64,64]{0,1:T(8,128)S(1)} all-gather(s32[64,16]{0,1:T(8,128)S(1)} %copy.57), channel_id=1, replica_groups=mesh['row'=8,'col'=4] {'col'}, dimensions={1}, use_global_device_ids=true | all-gather | bytes 20480 | tf_op jit(solution)/shard_map/all_gather | solution.py:194
  1086.7 8.0 scatter_custom_fusion.1
  1094.7 8.3 scatter_custom_fusion
  1103.0 7.6 broadcast_select_fusion.2
  1114.4 27.4 %gather_fusion.3 = f32[1024,2,1024]{2,1,0:T(2,128)} fusion(f32[4096,2,1024]{2,1,0:T(2,128)} %bitcast.7, s32[1024]{0:T(1024)S(1)} %broadcast_clamp_fusion), kind=kCustom, calls=%fused_computation.3 | custom fusion | bytes 16781312 | tf_op jit(solution)/shard_map/jit(_take)/gather | solution.py:187
  1141.8 11.5 fusion.42
  1153.2 11.0 copy.71
  1164.2 27.4 %gather_fusion.2 = f32[1024,2,1024]{2,1,0:T(2,128)} fusion(f32[4096,2,1024]{2,1,0:T(2,128)} %bitcast.7, s32[1024]{0:T(1024)S(1)} %broadcast_clamp_fusion.1), kind=kCustom, calls=%fused_computation.2 | custom fusion | bytes 16781312 | tf_op jit(solution)/shard_map/jit(_take)/gather | solution.py:187
  1191.6 11.5 fusion.41
  1203.0 11.0 copy.73
  1214.3 13.0 fusion.19
  1227.4 7.6 fusion.4
  1235.0 8.7 convolution_add_fusion.2
  1247.8 11.0 copy.77
  1258.8 11.0 copy.76
  1270.1 11.6 fusion.21
  1281.7 7.0 fusion
  1288.7 7.4 fusion.45
  1302.6 134.0 %reduce-scatter.3.cloned.1.call-done = f32[256,1024]{1,0:T(8,128)} async-done(((f32[1024,1024]{1,0:T(8,128)}), f32[256,1024]{1,0:T(8,128)}) %reduce-scatter.3.cloned.1.call-update) | async-done | bytes 1048592 | tf_op jit(solution)/shard_map/reduce_scatter | solution.py:231
  1439.0 52.7 %all-gather.5.cloned.1.call-done = f32[1024,1024]{1,0:T(8,128)} async-done(((f32[256,1024]{1,0:T(8,128)}), f32[1024,1024]{1,0:T(8,128)}) %all-gather.5.cloned.1.call-update) | async-done | bytes 4194320 | tf_op jit(solution)/shard_map/all_gather | solution.py:233
  1497.0 7.3 fusion.8
  1504.4 7.3 convolution_add_fusion.1
  1511.7 28.9 %collective-permute-done.3 = f32[1024,1024]{1,0:T(8,128)S(1)} collective-permute-done((f32[1024,1024]{1,0:T(8,128)}, f32[1024,1024]{1,0:T(8,128)S(1)}, u32[]{:S(2)}, u32[]{:S(2)}) %collective-permute-start.3) | collective-permute-done | bytes 4194336 | tf_op jit(solution)/shard_map/ppermute | solution.py:234
  1541.2 6.7 fusion.12
  1548.0 7.9 broadcast_select_fusion.1
  1556.0 49.8 %collective-permute-done.4 = f32[1024,1024]{1,0:T(8,128)S(1)} collective-permute-done((f32[1024,1024]{1,0:T(8,128)S(1)}, f32[1024,1024]{1,0:T(8,128)S(1)}, u32[]{:S(2)}, u32[]{:S(2)}) %collective-permute-start.4) | collective-permute-done | bytes 4194336 | tf_op jit(solution)/shard_map/ppermute | solution.py:237
  1609.8 225.6 %reduce-scatter.5.cloned.1.call-done = f32[256,1024]{1,0:T(8,128)} async-done(((f32[1024,1024]{1,0:T(8,128)}), f32[256,1024]{1,0:T(8,128)}) %reduce-scatter.5.cloned.1.call-update) | async-done | bytes 1048592 | tf_op jit(solution)/shard_map/reduce_scatter | solution.py:239
  1838.5 37.2 %collective-permute-done.5 = f32[256,1024]{1,0:T(8,128)S(1)} collective-permute-done((f32[256,1024]{1,0:T(8,128)}, f32[256,1024]{1,0:T(8,128)S(1)}, u32[]{:S(2)}, u32[]{:S(2)}) %collective-permute-start.5) | collective-permute-done | bytes 1048608 | tf_op jit(solution)/shard_map/ppermute | solution.py:240
  (118 shorter events, 57.3 us)
Async XLA Ops:
  14.3 48.2 %all-to-all-start.1 = ((s32[32,1,128]{2,1,0:T(1,128)}), s32[32,1,128]{2,1,0:T(1,128)S(1)}, u32[]{:S(2)}, u32[]{:S(2)}) async-start(s32[32,1,128]{2,1,0:T(1,128)} %reshape.245), calls=%async_computation.1 | async-start | bytes 32768 | tf_op jit(solution)/shard_map/all_to_all | solution.py:176
  62.5 4.3 copy-start.15
  62.5 1051.9 %all-to-all-start = ((f32[32,2,64,2,1024]{4,3,2,1,0:T(2,128)}), f32[32,2,64,2,1024]{4,3,2,1,0:T(2,128)}, u32[]{:S(2)}, u32[]{:S(2)}) async-start(f32[32,2,64,2,1024]{4,3,2,1,0:T(2,128)} %bitcast.115), calls=%async_computation | async-start | bytes 67108864 | tf_op jit(solution)/shard_map/all_to_all | solution.py:178
  66.7 866.4 %copy-start.20 = (s32[32]{0:T(128)S(1)}, s32[32]{0:T(128)}, u32[]{:S(2)}) copy-start(s32[32]{0:T(128)} %constant.63.clone) | copy-start | bytes 388
  66.7 867.6 %copy-start.21 = (pred[32]{0:T(512)(128)(4,1)S(1)}, pred[32]{0:T(512)(128)(4,1)}, u32[]{:S(2)}) copy-start(pred[32]{0:T(512)(128)(4,1)} %constant.64.clone) | copy-start | bytes 100
  66.7 871.4 %copy-start.17 = (s32[8,16]{1,0:T(8,128)S(1)}, s32[8,16]{1,0:T(8,128)}, u32[]{:S(2)}) copy-start(s32[8,16]{1,0:T(8,128)} %param.14) | copy-start | bytes 1540
  66.7 863.7 %all-gather.3.cloned.1.call-start = ((), (), s32[]{:S(2)}) async-start(), calls=%async_computation.4 | async-start | bytes 5242880 | tf_op jit(solution)/shard_map/all_gather | solution.py:215
  66.9 575.7 %collective-permute-start = (f32[256,1024]{1,0:T(8,128)S(1)}, f32[256,1024]{1,0:T(8,128)S(1)}, u32[]{:S(2)}, u32[]{:S(2)}) collective-permute-start(f32[256,1024]{1,0:T(8,128)S(1)} %pad_maximum_fusion), channel_id=1, source_target_pairs={{0,0},{4,1},{8,2},{12,3},{16,4},{20,5},{24,6},{28,7},{1,8},{5,9},{... | collective-permute-start | bytes 3145736 | tf_op jit(solution)/shard_map/ppermute | solution.py:214
  642.7 1.0 copy-start.16
  643.7 792.9 %reduce-scatter.3.cloned.1.call-start = ((), (), s32[]{:S(2)}) async-start(), calls=%async_computation.5 | async-start | bytes 5242880 | tf_op jit(solution)/shard_map/reduce_scatter | solution.py:231
  930.5 172.6 %collective-permute-start.1 = (f32[1024,1024]{1,0:T(8,128)}, f32[1024,1024]{1,0:T(8,128)}, u32[]{:S(2)}, u32[]{:S(2)}) collective-permute-start(f32[1024,1024]{1,0:T(8,128)} %all-gather.3.cloned.1.call-done), channel_id=1, source_target_pairs={{16,0},{5,1},{10,2},{15,3},{0,4},{9,5},{14,6},{19,7},{24,8},{13,9}... | collective-permute-start | bytes 12582920 | tf_op jit(solution)/shard_map/ppermute | solution.py:216
  1110.6 2.0 copy-start.1
  1214.3 13.1 copy-start.13
  1227.4 7.6 copy-start.5
  1227.4 7.6 copy-start.3
  1227.4 7.6 copy-start.2
  1243.7 52.5 %collective-permute-start.2 = (f32[1024,1024]{1,0:T(8,128)}, f32[1024,1024]{1,0:T(8,128)}, u32[]{:S(2)}, u32[]{:S(2)}) collective-permute-start(f32[1024,1024]{1,0:T(8,128)} %convolution_add_fusion.2), channel_id=1, source_target_pairs={{0,16},{1,5},{2,10},{3,15},{4,0},{5,9},{6,14},{7,19},{8,24},{9,13}... | collective-permute-start | bytes 12582920 | tf_op jit(solution)/shard_map/ppermute | solution.py:229
  1270.1 11.6 copy-start.14
  1281.6 7.0 copy-start.9
  1281.7 7.0 copy-start.7
  1281.7 7.0 copy-start
  1301.8 189.8 %all-gather.5.cloned.1.call-start = ((), (), s32[]{:S(2)}) async-start(), calls=%async_computation.6 | async-start | bytes 5242880 | tf_op jit(solution)/shard_map/all_gather | solution.py:233
  1438.9 396.5 %reduce-scatter.5.cloned.1.call-start = ((), (), s32[]{:S(2)}) async-start(), calls=%async_computation.7 | async-start | bytes 5242880 | tf_op jit(solution)/shard_map/reduce_scatter | solution.py:239
  1491.7 5.3 copy-start.10
  1491.7 48.9 %collective-permute-start.3 = (f32[1024,1024]{1,0:T(8,128)}, f32[1024,1024]{1,0:T(8,128)S(1)}, u32[]{:S(2)}, u32[]{:S(2)}) collective-permute-start(f32[1024,1024]{1,0:T(8,128)} %all-gather.5.cloned.1.call-done), channel_id=1, source_target_pairs={{16,0},{5,1},{10,2},{15,3},{0,4},{9,5},{14,6},{19,7},{24,8},{13,9}... | collective-permute-start | bytes 12582920 | tf_op jit(solution)/shard_map/ppermute | solution.py:234
  1497.0 7.4 copy-start.8
  1497.0 7.4 copy-start.11
  1511.7 29.5 %copy-start.6 = (f32[1024,1024]{0,1:T(8,128)S(1)}, f32[1024,1024]{0,1:T(8,128)}, u32[]{:S(2)}) copy-start(f32[1024,1024]{0,1:T(8,128)} %copy-done.5) | copy-start | bytes 12582916
  1541.2 6.8 copy-start.4
  1555.9 49.8 %collective-permute-start.4 = (f32[1024,1024]{1,0:T(8,128)S(1)}, f32[1024,1024]{1,0:T(8,128)S(1)}, u32[]{:S(2)}, u32[]{:S(2)}) collective-permute-start(f32[1024,1024]{1,0:T(8,128)S(1)} %get-tuple-element.36), channel_id=1, source_target_pairs={{0,16},{1,5},{2,10},{3,15},{4,0},{5,9},{6,14},{7,19},{8,24},{9,13}... | collective-permute-start | bytes 12582920 | tf_op jit(solution)/shard_map/ppermute | solution.py:237
  1609.8 227.5 %copy-start.12 = (f32[256,1024]{1,0:T(8,128)S(1)}, f32[256,1024]{1,0:T(8,128)}, u32[]{:S(2)}) copy-start(f32[256,1024]{1,0:T(8,128)} %reduce-scatter.3.cloned.1.call-done) | copy-start | bytes 3145732
  1835.4 40.3 %collective-permute-start.5 = (f32[256,1024]{1,0:T(8,128)}, f32[256,1024]{1,0:T(8,128)S(1)}, u32[]{:S(2)}, u32[]{:S(2)}) collective-permute-start(f32[256,1024]{1,0:T(8,128)} %reduce-scatter.5.cloned.1.call-done), channel_id=1, source_target_pairs={{0,0},{1,4},{2,8},{3,12},{4,16},{5,20},{6,24},{7,28},{8,1},{9,5},{... | collective-permute-start | bytes 3145736 | tf_op jit(solution)/shard_map/ppermute | solution.py:240
  (2 other events, 1.4 us)
Sparse Core Ops, SparseCore 0:
  643.8 286.6 all-gather.2
  1302.0 134.5 reduce-scatter.2
  1439.1 52.5 all-gather.4
  1610.0 225.4 reduce-scatter.4

commit v2 on v1

--- a/solution.py
+++ b/solution.py
@@ -8,10 +8,13 @@
 from jax.sharding import PartitionSpec as P
 
 AXES = ("row", "col")
+PIECES = 2
 
 
 def partner(i, j, rows):
     half = rows // 2
+    if j % 2:
+        return (i + (j ^ 2 if i % 2 else j)) % rows
     if j:
         return (i + j) % rows
     if i < half:
@@ -152,7 +155,7 @@
     focus = focus_panel.shape[2]
     rows = lax.axis_size("row")
     cols = lax.axis_size("col")
-    assert rows == 2 * cols and rows % 4 == 0
+    assert rows == 2 * cols and cols % 4 == 0
     devices = rows * cols
     width = stations // rows
     cap = slot_total // rows
@@ -173,11 +176,36 @@
         [by_group[jnp.asarray(firsts, jnp.int32)], by_group[jnp.asarray(seconds, jnp.int32)]],
         axis=1,
     )
-    labels = lax.all_to_all(label_out, AXES, split_axis=0, concat_axis=0, tiled=True)
+    blocks_down, blocks_across = missing_blocks.shape
+    note_size = blocks_down * blocks_across
+    panel = jnp.concatenate([focus_panel[0], focus_panel[1]], axis=1)
+    panel = lax.ppermute(panel, AXES, to_row_major)
     packed = pack(shot_traces, source, table, cap, width)
+    outgoing = jnp.concatenate(
+        [
+            label_out.reshape(devices, 2 * cap),
+            jnp.broadcast_to(missing_blocks.reshape(1, note_size), (devices, note_size)),
+        ],
+        axis=1,
+    )
+    packed, outgoing, panel = lax.optimization_barrier((packed, outgoing, panel))
+    notes = lax.all_to_all(outgoing, AXES, split_axis=0, concat_axis=0, tiled=True)
+    packed, notes = lax.optimization_barrier((packed, notes))
+    panel_first = lax.all_gather(panel, "col", axis=0, tiled=True)
+    labels = notes[:, : 2 * cap].reshape(devices, 2, cap)
+    missing = (
+        notes[:, 2 * cap :]
+        .reshape(rows, cols, blocks_down, blocks_across)
+        .transpose(0, 2, 1, 3)
+        .reshape(rows * blocks_down, cols * blocks_across)
+    )
+
     arrived = lax.all_to_all(
         packed.reshape(devices, 2, cap, 2, width), AXES, split_axis=0, concat_axis=0, tiled=True
-    ).reshape(devices * 2 * cap, 2, width)
+    )
+    arrived, panel_sent = lax.optimization_barrier((arrived, panel_first))
+    panel_second = lax.ppermute(panel_sent, AXES, from_partner)
+    arrived = arrived.reshape(devices * 2 * cap, 2, width)
     indices = jnp.arange(devices * 2 * cap, dtype=jnp.int32).reshape(devices, 2, cap)
 
     def block(q, group):
@@ -190,8 +218,6 @@
     re0, im0 = block(0, first)
     re1, im1 = block(1, second)
 
-    missing = lax.all_gather(missing_blocks, "row", axis=0, tiled=True)
-    missing = lax.all_gather(missing, "col", axis=1, tiled=True)
     blocks = missing.shape[0] // rows
     side = width // blocks
 
@@ -210,38 +236,49 @@
     full_re0, full_im0 = fill(mask0, re0, re1), fill(mask0, im0, im1)
     full_re1, full_im1 = fill(mask1, re1, re0), fill(mask1, im1, im0)
 
-    panel = jnp.concatenate([focus_panel[0], focus_panel[1]], axis=1)
-    panel = lax.ppermute(panel, AXES, to_row_major)
-    panel_first = lax.all_gather(panel, "col", axis=0, tiled=True)
-    panel_second = lax.ppermute(panel_first, AXES, from_partner)
-
     def forward(re, im, vec):
-        turned = jnp.concatenate([-vec[:, focus:], vec[:, :focus]], axis=1)
+        turned = jnp.concatenate([-vec[:, half:], vec[:, :half]], axis=1)
         return dot(re, vec) + dot(im, turned)
 
     def backward(re, im, vec):
-        turned = jnp.concatenate([vec[:, focus:], -vec[:, :focus]], axis=1)
+        turned = jnp.concatenate([vec[:, half:], -vec[:, :half]], axis=1)
         return trans_dot(re, vec) + trans_dot(im, turned)
 
-    field_second = forward(
-        full_re1, full_im1, jnp.where(diagonal, panel_second, panel_first)
-    )
-    field_moved = lax.ppermute(field_second, AXES, to_partner)
-    field_first = forward(full_re0, full_im0, jnp.where(diagonal, panel_first, panel_second))
-    own = lax.psum_scatter(field_first + field_moved, "col", scatter_dimension=0, tiled=True)
-    weighted = own * lookup(weight_bins, weight_table)[:, None]
-    weighted_first = lax.all_gather(weighted, "col", axis=0, tiled=True)
-    weighted_second = lax.ppermute(weighted_first, AXES, from_partner)
-    image0 = backward(full_re0, full_im0, weighted_first)
-    image1 = backward(full_re1, full_im1, weighted_second)
-    image_moved = lax.ppermute(jnp.where(diagonal, image1, image0), AXES, to_partner)
-    image_sum = jnp.where(diagonal, image0, image1) + image_moved
-    image = lax.psum_scatter(image_sum, "col", scatter_dimension=0, tiled=True)
-    image = lax.ppermute(image, AXES, to_col_major)
-    return (
-        jnp.stack([own[:, :focus], own[:, focus:]]),
-        jnp.stack([image[:, :focus], image[:, focus:]]),
-    )
+    def part(vec, h):
+        lo = h * half
+        return jnp.concatenate([vec[:, lo : lo + half], vec[:, focus + lo : focus + lo + half]], 1)
+
+    half = focus // PIECES
+    weights = lookup(weight_bins, weight_table)[:, None]
+    vec1 = jnp.where(diagonal, panel_second, panel_first)
+    vec0 = jnp.where(diagonal, panel_first, panel_second)
+    moved = [
+        lax.ppermute(forward(full_re1, full_im1, part(vec1, h)), AXES, to_partner)
+        for h in range(PIECES)
+    ]
+    owns, images = [], []
+    for h in range(PIECES):
+        field = forward(full_re0, full_im0, part(vec0, h)) + moved[h]
+        own = lax.psum_scatter(field, "col", scatter_dimension=0, tiled=True)
+        owns.append(own)
+        weighted_first = lax.all_gather(own * weights, "col", axis=0, tiled=True)
+        weighted_second = lax.ppermute(weighted_first, AXES, from_partner)
+        image0 = backward(full_re0, full_im0, weighted_first)
+        image1 = backward(full_re1, full_im1, weighted_second)
+        image_moved = lax.ppermute(jnp.where(diagonal, image1, image0), AXES, to_partner)
+        image = jnp.where(diagonal, image0, image1) + image_moved
+        image = lax.psum_scatter(image, "col", scatter_dimension=0, tiled=True)
+        images.append(lax.ppermute(image, AXES, to_col_major))
+
+    def join(pieces):
+        return jnp.stack(
+            [
+                jnp.concatenate([piece[:, :half] for piece in pieces], axis=1),
+                jnp.concatenate([piece[:, half:] for piece in pieces], axis=1),
+            ]
+        )
+
+    return join(owns), join(images)
 
 
 def solution(mesh):

time: 1890 us -> 1550 us (0.82)
  waiting for transfers between devices: 1390 us -> 1070 us
  blocking collectives: 147 us -> 43.8 us
  starting transfers between devices: 19.6 us -> 82.7 us
  matrix products: 59.9 us -> 88.1 us
    ppermute x1, waiting for transfers between devices: 574 us -> 0.01 us  [local(): panel = lax.ppermute(panel, AXES, to_row_major)]
    all_to_all x1, waiting for transfers between devices: 0.01 us -> 528 us  [local(): lax.all_to_all(packed.reshape(devices, 2, cap, 2, width), AXES, split_axi...]
    reduce_scatter x2 -> x4, waiting for transfers between devices: 360 us -> 128 us  [the longest x2 85 us: local(): image = lax.psum_scatter(image, 'col', scatter_dimension=0, tiled=True)]
    all_gather x2 -> x0, blocking collectives: 147 us -> none  [the longest x1 96 us: local(): missing = lax.all_gather(missing, 'col', axis=1, tiled=True)]
    ppermute x1 -> x2, starting transfers between devices: 0.06 us -> 66.9 us  [local(): lax.ppermute(jnp.where(diagonal, image1, image0), AXES, to_partner)]
    all_to_all x0 -> x1, blocking collectives: none -> 43.8 us  [local(): lax.all_to_all(outgoing, AXES, split_axis=0, concat_axis=0, tiled=True)]
    ppermute x1 -> x2, waiting for transfers between devices: 49.8 us -> 22.9 us  [local(): lax.ppermute(jnp.where(diagonal, image1, image0), AXES, to_partner)]
    all_gather x1, waiting for transfers between devices: 287 us -> 262 us  [local(): panel_first = lax.all_gather(panel, 'col', axis=0, tiled=True)]
  transfers between devices with their start and end apart: 12 -> 18, of which waited for: 8 -> 12; matrix products, arithmetic and copies ran while one was open for 5% -> 16% of each run, Pallas kernels for 2% -> 2%
where the time goes in v2:
time: 1550 us; the launch traced here: 1540 us
  waiting for transfers between devices  1070 us (69%)
  local copies, waits for them, and re-layouts  147 us (9%)
  matrix products  88.1 us (6%)
  starting transfers between devices  82.7 us (5%)
  other arithmetic  58.6 us (4%)
  blocking collectives  43.8 us (3%)
  Pallas kernels  31.1 us (2%)
  between operations  19.7 us (1%)
    all_to_all x1, waiting for transfers between devices, local(): lax.all_to_all(packed.reshape(devices, 2, cap, 2, width), AXES, split_axi...  528 us
    all_gather x1, waiting for transfers between devices, local(): panel_first = lax.all_gather(panel, 'col', axis=0, tiled=True)  262 us
    reduce_scatter x2, waiting for transfers between devices, local(): image = lax.psum_scatter(image, 'col', scatter_dimension=0, tiled=True)  85 us
    ppermute x2, starting transfers between devices, local(): lax.ppermute(jnp.where(diagonal, image1, image0), AXES, to_partner)  66.9 us
    gather x2, local copies, waits for them, and re-layouts, block(): taken = jnp.take(arrived, where_from, axis=0, mode='clip')  54.7 us
    dot_general x8, matrix products, dot(): jnp.dot(left, right, precision=lax.Precision.HIGH, preferred_element_type...  49.2 us
    all_to_all x1, blocking collectives, local(): lax.all_to_all(outgoing, AXES, split_axis=0, concat_axis=0, tiled=True)  43.8 us
    reduce_scatter x2, waiting for transfers between devices, local(): own = lax.psum_scatter(field, 'col', scatter_dimension=0, tiled=True)  42.7 us
  transfers between devices with their start and end apart: 18, of which 12 were waited for; matrix products, arithmetic and copies ran while one was open for 16% of the time, Pallas kernels for 2%

profile of v2, /device:TPU:2, one launch (start us, length us, event | category | flops | bytes accessed | tf_op | source)
XLA Modules:
  0.0 1539.8 jit_solution(1023289181792721919)
XLA Ops:
  17.1 31.1 %shard_map.122 = f32[64,64,2,1024]{3,2,1,0:T(2,128)} custom-call(s32[512]{0:T(512)} %get-tuple-element.21.src_ref, f32[512,2,8192]{2,1,0:T(2,128)} %x_ref.1), custom_call_target="tpu_custom_call" | custom-call | tf_op jit(solution)/shard_map/pallas_call | solution.py:105
  48.3 43.8 %all_to_all.17 = s32[32,1,256]{2,1,0:T(1,128)S(1)} all-to-all(s32[32,1,256]{2,1,0:T(1,128)S(1)} %copy.65), channel_id=1, replica_groups=mesh['row'=8,'col'=4] {'row','col'}, dimensions={0} | all-to-all | bytes 65536 | tf_op jit(solution)/shard_map/all_to_all | solution.py:192
  104.3 262.4 %all-gather.4.cloned.1.call-done = f32[1024,1024]{0,1:T(8,128)} async-done(((f32[256,1024]{0,1:T(8,128)}), f32[1024,1024]{0,1:T(8,128)}) %all-gather.4.cloned.1.call-update) | async-done | bytes 4194320 | tf_op jit(solution)/shard_map/all_gather | solution.py:194
  366.7 527.9 %all-to-all-done.1 = f32[32,2,64,2,1024]{4,3,2,1,0:T(2,128)} async-done(((f32[32,2,64,2,1024]{4,3,2,1,0:T(2,128)}), f32[32,2,64,2,1024]{4,3,2,1,0:T(2,128)}, u32[]{:S(2)}, u32[]{:S(2)}) %all-to-all-start.1) | async-done | bytes 33554464 | tf_op jit(solution)/shard_map/all_to_all | solution.py:203
  894.8 8.0 scatter_custom_fusion.1
  902.8 8.3 scatter_custom_fusion
  911.2 27.3 %gather_fusion.3 = f32[1024,2,1024]{2,1,0:T(2,128)} fusion(f32[4096,2,1024]{2,1,0:T(2,128)} %bitcast.13, s32[1024]{0:T(1024)S(1)} %broadcast_clamp_fusion), kind=kCustom, calls=%fused_computation.3 | custom fusion | bytes 16781312 | tf_op jit(solution)/shard_map/jit(_take)/gather | solution.py:215
  938.5 11.5 fusion.88
  950.0 11.0 copy.81
  961.0 27.3 %gather_fusion.2 = f32[1024,2,1024]{2,1,0:T(2,128)} fusion(f32[4096,2,1024]{2,1,0:T(2,128)} %bitcast.13, s32[1024]{0:T(1024)S(1)} %broadcast_clamp_fusion.1), kind=kCustom, calls=%fused_computation.2 | custom fusion | bytes 16781312 | tf_op jit(solution)/shard_map/jit(_take)/gather | solution.py:215
  988.3 10.9 copy.83
  999.2 9.7 fusion.87
  1009.3 11.8 fusion.3
  1021.1 9.8 broadcast_select_fusion.1
  1032.6 6.8 fusion.36
  1039.4 8.4 fusion.56
  1048.3 11.0 copy.87
  1059.2 11.0 copy.86
  1070.6 11.4 fusion.5
  1088.2 8.7 collective-permute-done.3
  1103.3 9.2 fusion.20
  1123.2 22.8 %collective-permute-done.2 = f32[1024,512]{1,0:T(8,128)S(1)} collective-permute-done((f32[1024,512]{1,0:T(8,128)S(1)}, f32[1024,512]{1,0:T(8,128)S(1)}, u32[]{:S(2)}, u32[]{:S(2)}) %collective-permute-start.2) | collective-permute-done | bytes 2097184 | tf_op jit(solution)/shard_map/ppermute | solution.py:256
  1151.7 42.7 %reduce-scatter.5.cloned.1.call-done = f32[256,512]{1,0:T(8,128)} async-done(((f32[1024,512]{1,0:T(8,128)}), f32[256,512]{1,0:T(8,128)}) %reduce-scatter.5.cloned.1.call-update) | async-done | bytes 524304 | tf_op jit(solution)/shard_map/reduce_scatter | solution.py:262
  1196.8 35.3 %all-gather.8.cloned.1.call-done = f32[1024,512]{1,0:T(8,128)} async-done(((f32[256,512]{1,0:T(8,128)}), f32[1024,512]{1,0:T(8,128)}) %all-gather.8.cloned.1.call-update) | async-done | bytes 2097168 | tf_op jit(solution)/shard_map/all_gather | solution.py:264
  1244.0 13.7 collective-permute-done.7
  1263.0 7.7 broadcast_select_fusion.2
  1270.7 30.0 %collective-permute-start.8 = (f32[1024,512]{1,0:T(8,128)}, f32[1024,512]{1,0:T(8,128)}, u32[]{:S(2)}, u32[]{:S(2)}) collective-permute-start(f32[1024,512]{1,0:T(8,128)} %get-tuple-element.70), channel_id=1, source_target_pairs={{0,16},{1,5},{2,10},{3,15},{4,0},{5,17},{6,14},{7,11},{8,24},{9,13... | collective-permute-start | bytes 6291464 | tf_op jit(solution)/shard_map/ppermute | solution.py:268
  1320.5 25.9 %collective-permute-done.4 = f32[1024,512]{1,0:T(8,128)} collective-permute-done((f32[1024,512]{1,0:T(8,128)}, f32[1024,512]{1,0:T(8,128)}, u32[]{:S(2)}, u32[]{:S(2)}) %collective-permute-start.4) | collective-permute-done | bytes 2097184 | tf_op jit(solution)/shard_map/ppermute | solution.py:265
  1357.5 37.0 %collective-permute-start.5 = (f32[1024,512]{1,0:T(8,128)S(1)}, f32[1024,512]{1,0:T(8,128)S(1)}, u32[]{:S(2)}, u32[]{:S(2)}) collective-permute-start(f32[1024,512]{1,0:T(8,128)S(1)} %get-tuple-element.72), channel_id=1, source_target_pairs={{0,16},{1,5},{2,10},{3,15},{4,0},{5,17},{6,14},{7,11},{8,24},{9,13... | collective-permute-start | bytes 6291464 | tf_op jit(solution)/shard_map/ppermute | solution.py:268
  1394.5 22.9 %collective-permute-done.5 = f32[1024,512]{1,0:T(8,128)S(1)} collective-permute-done((f32[1024,512]{1,0:T(8,128)S(1)}, f32[1024,512]{1,0:T(8,128)S(1)}, u32[]{:S(2)}, u32[]{:S(2)}) %collective-permute-start.5) | collective-permute-done | bytes 2097184 | tf_op jit(solution)/shard_map/ppermute | solution.py:268
  1429.7 78.4 %reduce-scatter.9.cloned.1.call-done = f32[256,512]{1,0:T(8,128)} async-done(((f32[1024,512]{1,0:T(8,128)}), f32[256,512]{1,0:T(8,128)}) %reduce-scatter.9.cloned.1.call-update) | async-done | bytes 524304 | tf_op jit(solution)/shard_map/reduce_scatter | solution.py:270
  1511.2 20.3 %collective-permute-done.6 = f32[256,512]{1,0:T(8,128)S(1)} collective-permute-done((f32[256,512]{1,0:T(8,128)}, f32[256,512]{1,0:T(8,128)S(1)}, u32[]{:S(2)}, u32[]{:S(2)}) %collective-permute-start.6) | collective-permute-done | bytes 524320 | tf_op jit(solution)/shard_map/ppermute | solution.py:271
  (178 shorter events, 116.1 us)
Async XLA Ops:
  9.0 39.3 %collective-permute-start = (f32[256,1024]{0,1:T(8,128)S(1)}, f32[256,1024]{0,1:T(8,128)S(1)}, u32[]{:S(2)}, u32[]{:S(2)}) collective-permute-start(f32[256,1024]{0,1:T(8,128)S(1)} %pad_maximum_fusion), channel_id=1, source_target_pairs={{0,0},{4,1},{8,2},{12,3},{16,4},{20,5},{24,6},{28,7},{1,8},{5,9},{... | collective-permute-start | bytes 3145736 | tf_op jit(solution)/shard_map/ppermute | solution.py:182
  48.2 43.8 %copy-start.25 = (f32[256,1024]{0,1:T(8,128)}, f32[256,1024]{0,1:T(8,128)S(1)}, u32[]{:S(2)}) copy-start(f32[256,1024]{0,1:T(8,128)S(1)} %collective-permute-done) | copy-start | bytes 3145732
  92.1 802.5 %all-to-all-start.1 = ((f32[32,2,64,2,1024]{4,3,2,1,0:T(2,128)}), f32[32,2,64,2,1024]{4,3,2,1,0:T(2,128)}, u32[]{:S(2)}, u32[]{:S(2)}) async-start(f32[32,2,64,2,1024]{4,3,2,1,0:T(2,128)} %bitcast.123), calls=%async_computation.1 | async-start | bytes 67108864 | tf_op jit(solution)/shard_map/all_to_all | solution.py:203
  97.5 269.2 %all-gather.4.cloned.1.call-start = ((), (), s32[]{:S(2)}) async-start(), calls=%async_computation.6 | async-start | bytes 5242880 | tf_op jit(solution)/shard_map/all_gather | solution.py:194
  98.2 1053.5 %reduce-scatter.7.cloned.1.call-start = ((), (), s32[]{:S(2)}) async-start(), calls=%async_computation.8 | async-start | bytes 2621440 | tf_op jit(solution)/shard_map/reduce_scatter | solution.py:262
  894.6 126.5 %collective-permute-start.1 = (f32[1024,1024]{0,1:T(8,128)}, f32[1024,1024]{0,1:T(8,128)}, u32[]{:S(2)}, u32[]{:S(2)}) collective-permute-start(f32[1024,1024]{0,1:T(8,128)} %all-gather.4.cloned.1.call-done), channel_id=1, source_target_pairs={{16,0},{5,1},{10,2},{15,3},{0,4},{17,5},{14,6},{11,7},{24,8},{13,9... | collective-permute-start | bytes 12582920 | tf_op jit(solution)/shard_map/ppermute | solution.py:207
  999.2 10.0 copy-start.16
  1008.9 12.2 copy-start.14
  1008.9 12.2 copy-start.15
  1021.1 11.5 copy-start
  1021.1 18.3 %copy-start.7 = (f32[1024,1024]{0,1:T(8,128)}, f32[1024,1024]{0,1:T(8,128)S(1)}, u32[]{:S(2)}) copy-start(f32[1024,1024]{0,1:T(8,128)S(1)} %get-tuple-element.50) | copy-start | bytes 12582916
  1047.8 49.1 %collective-permute-start.3 = (f32[1024,512]{1,0:T(8,128)}, f32[1024,512]{1,0:T(8,128)}, u32[]{:S(2)}, u32[]{:S(2)}) collective-permute-start(f32[1024,512]{1,0:T(8,128)} %fusion.56), channel_id=1, source_target_pairs={{0,16},{1,5},{2,10},{3,15},{4,0},{5,17},{6,14},{7,11},{8,24},{9,13... | collective-permute-start | bytes 6291464 | tf_op jit(solution)/shard_map/ppermute | solution.py:256
  1070.6 11.5 copy-start.17
  1082.0 14.9 copy-start.11
  1103.3 91.2 %reduce-scatter.5.cloned.1.call-start = ((), (), s32[]{:S(2)}) async-start(), calls=%async_computation.7 | async-start | bytes 2621440 | tf_op jit(solution)/shard_map/reduce_scatter | solution.py:262
  1103.3 9.2 copy-start.8
  1119.3 26.8 %collective-permute-start.2 = (f32[1024,512]{1,0:T(8,128)S(1)}, f32[1024,512]{1,0:T(8,128)S(1)}, u32[]{:S(2)}, u32[]{:S(2)}) collective-permute-start(f32[1024,512]{1,0:T(8,128)S(1)} %fusion.59), channel_id=1, source_target_pairs={{0,16},{1,5},{2,10},{3,15},{4,0},{5,17},{6,14},{7,11},{8,24},{9,13... | collective-permute-start | bytes 6291464 | tf_op jit(solution)/shard_map/ppermute | solution.py:256
  1119.7 26.3 %copy-start.12 = (f32[1024,1024]{1,0:T(8,128)S(1)}, f32[1024,1024]{1,0:T(8,128)}, u32[]{:S(2)}) copy-start(f32[1024,1024]{1,0:T(8,128)} %copy-done.11) | copy-start | bytes 12582916
  1119.8 26.3 %copy-start.21 = (f32[1024,256]{0,1:T(8,128)S(1)}, f32[1024,256]{0,1:T(8,128)}, u32[]{:S(2)}) copy-start(f32[1024,256]{0,1:T(8,128)} %get-tuple-element.32) | copy-start | bytes 3145732
  1151.0 81.1 %all-gather.8.cloned.1.call-start = ((), (), s32[]{:S(2)}) async-start(), calls=%async_computation.11 | async-start | bytes 2621440 | tf_op jit(solution)/shard_map/all_gather | solution.py:264
  1196.8 103.8 %all-gather.6.cloned.1.call-start = ((), (), s32[]{:S(2)}) async-start(), calls=%async_computation.9 | async-start | bytes 2621440 | tf_op jit(solution)/shard_map/all_gather | solution.py:264
  1232.1 25.6 %collective-permute-start.7 = (f32[1024,512]{1,0:T(8,128)}, f32[1024,512]{1,0:T(8,128)}, u32[]{:S(2)}, u32[]{:S(2)}) collective-permute-start(f32[1024,512]{1,0:T(8,128)} %all-gather.8.cloned.1.call-done), channel_id=1, source_target_pairs={{16,0},{5,1},{10,2},{15,3},{0,4},{17,5},{14,6},{11,7},{24,8},{13,9... | collective-permute-start | bytes 6291464 | tf_op jit(solution)/shard_map/ppermute | solution.py:265
  1233.8 193.9 %reduce-scatter.11.cloned.1.call-start = ((), (), s32[]{:S(2)}) async-start(), calls=%async_computation.12 | async-start | bytes 2621440 | tf_op jit(solution)/shard_map/reduce_scatter | solution.py:270
  1244.0 15.4 %copy-start.1 = (f32[1024,1024]{0,1:T(8,128)S(1)}, f32[1024,1024]{0,1:T(8,128)}, u32[]{:S(2)}) copy-start(f32[1024,1024]{0,1:T(8,128)} %copy-done) | copy-start | bytes 12582916
  1270.7 37.6 %collective-permute-start.8 = (f32[1024,512]{1,0:T(8,128)}, f32[1024,512]{1,0:T(8,128)}, u32[]{:S(2)}, u32[]{:S(2)}) collective-permute-start(f32[1024,512]{1,0:T(8,128)} %get-tuple-element.70), channel_id=1, source_target_pairs={{0,16},{1,5},{2,10},{3,15},{4,0},{5,17},{6,14},{7,11},{8,24},{9,13... | collective-permute-start | bytes 6291464 | tf_op jit(solution)/shard_map/ppermute | solution.py:268
  1300.6 45.7 %collective-permute-start.4 = (f32[1024,512]{1,0:T(8,128)}, f32[1024,512]{1,0:T(8,128)}, u32[]{:S(2)}, u32[]{:S(2)}) collective-permute-start(f32[1024,512]{1,0:T(8,128)} %all-gather.6.cloned.1.call-done), channel_id=1, source_target_pairs={{16,0},{5,1},{10,2},{15,3},{0,4},{17,5},{14,6},{11,7},{24,8},{13,9... | collective-permute-start | bytes 6291464 | tf_op jit(solution)/shard_map/ppermute | solution.py:265
  1312.6 195.5 %reduce-scatter.9.cloned.1.call-start = ((), (), s32[]{:S(2)}) async-start(), calls=%async_computation.10 | async-start | bytes 2621440 | tf_op jit(solution)/shard_map/reduce_scatter | solution.py:270
  1320.5 27.6 %copy-start.2 = (f32[1024,1024]{0,1:T(8,128)S(1)}, f32[1024,1024]{0,1:T(8,128)}, u32[]{:S(2)}) copy-start(f32[1024,1024]{0,1:T(8,128)} %copy-done) | copy-start | bytes 12582916
  1357.5 59.9 %collective-permute-start.5 = (f32[1024,512]{1,0:T(8,128)S(1)}, f32[1024,512]{1,0:T(8,128)S(1)}, u32[]{:S(2)}, u32[]{:S(2)}) collective-permute-start(f32[1024,512]{1,0:T(8,128)S(1)} %get-tuple-element.72), channel_id=1, source_target_pairs={{0,16},{1,5},{2,10},{3,15},{4,0},{5,17},{6,14},{7,11},{8,24},{9,13... | collective-permute-start | bytes 6291464 | tf_op jit(solution)/shard_map/ppermute | solution.py:268
  1420.1 9.5 copy-start.24
  1427.7 83.5 %collective-permute-start.9 = (f32[256,512]{1,0:T(8,128)}, f32[256,512]{1,0:T(8,128)S(1)}, u32[]{:S(2)}, u32[]{:S(2)}) collective-permute-start(f32[256,512]{1,0:T(8,128)} %reduce-scatter.11.cloned.1.call-done), channel_id=1, source_target_pairs={{0,0},{1,4},{2,8},{3,12},{4,16},{5,20},{6,24},{7,28},{8,1},{9,5},{... | collective-permute-start | bytes 1572872 | tf_op jit(solution)/shard_map/ppermute | solution.py:271
  1508.1 23.4 %collective-permute-start.6 = (f32[256,512]{1,0:T(8,128)}, f32[256,512]{1,0:T(8,128)S(1)}, u32[]{:S(2)}, u32[]{:S(2)}) collective-permute-start(f32[256,512]{1,0:T(8,128)} %reduce-scatter.9.cloned.1.call-done), channel_id=1, source_target_pairs={{0,0},{1,4},{2,8},{3,12},{4,16},{5,20},{6,24},{7,28},{8,1},{9,5},{... | collective-permute-start | bytes 1572872 | tf_op jit(solution)/shard_map/ppermute | solution.py:271
  (19 other events, 80.4 us)
Sparse Core Ops, SparseCore 0:
  100.7 265.9 all-gather.3
  1103.4 43.2 reduce-scatter.6
  1151.1 43.3 reduce-scatter.4
  1196.9 35.1 all-gather.7
  1234.4 35.1 all-gather.5
  1312.7 114.9 reduce-scatter.10
  1430.7 77.3 reduce-scatter.8
